TPU v7x, 32 devices: a whole 2x2x4 slice. The times are simulated.
32 devices in a mesh: tm: 4 (over z), height: 8 (over y, x, core).
Axes of the slice: x: 2, y: 2, z: 4, core: 2. Of those that a mesh axis runs over, the one named last changes fastest.
Arguments:
- queries: bfloat16 [16, 16, 16, 2560], P('tm', 'height'), may hold values from -64 to 64
- keys: bfloat16 [16, 16, 16, 2560], P('tm', 'height'), may hold values from -64 to 64
- values: bfloat16 [16, 16, 16, 2560], P('tm', 'height'), may hold values from -6 to 6
- tile_mask: int32 [4, 8, 2, 18], P('tm', 'height'), may hold values 0 or 1
- sink_frame: int32 [1], replicated, may hold values from 0 to 15
Outputs:
- attended: bfloat16 [16, 16, 16, 2560], P('tm', 'height')
All inputs are finite; a program needn't handle non-finite values. No bound on the sum of `tile_mask` on one device may be relied on, other than what follows from the above.
Results may differ from a plain program's by a relative error of at most 0.0041.
Values may be sent and summed in bfloat16 or wider, within the bound.
No kernel may reach another device: no remote copies, remote signals or barrier semaphores. Data moves between devices by JAX's collectives and lax.ppermute only.
A program may use at most 128 MiB of HBM per device.

v0:
```python
import math
import jax
import jax.numpy as jnp
from jax import lax
from jax.sharding import PartitionSpec as P

H = 20
HD = 128
TF = 4
TC = 8
masked_score = -1e30


def from_behind(value, axis, steps):
    count = lax.axis_size(axis)
    first, last = (max(0, -steps), min(count, count - steps))
    return lax.ppermute(value, axis, [(source, source + steps) for source in range(first, last)])


def with_halo(cells, sides, width):
    for axis, dim in sides:
        count = lax.axis_size(axis)
        ends = count - 1
        head = lax.slice_in_dim(cells, 0, width, axis=dim)
        tail = lax.slice_in_dim(cells, cells.shape[dim] - width, cells.shape[dim], axis=dim)
        cells = jnp.concatenate(
            [
                lax.ppermute(tail, axis, [(i, (i + 1) % count) for i in range(ends)]),
                cells,
                lax.ppermute(head, axis, [((i + 1) % count, i) for i in range(ends)]),
            ],
            axis=dim,
        )
    return cells


def from_root(x, axis, root):
    mine = lax.axis_index(axis) == root
    return lax.psum(jnp.where(mine, x, jnp.zeros_like(x)), axis)


def near_allowed(tile_flags, time_base, band_index, band_total):
    q_tiles = tile_flags.shape[0]
    w_tiles = tile_flags.shape[1]
    q_time = jnp.arange(q_tiles)[:, None, None, None, None]
    q_width = jnp.arange(w_tiles)[None, :, None, None, None]
    slot = jnp.arange(2)[None, None, :, None, None]
    k_band = jnp.arange(3)[None, None, None, :, None] - 1
    width_slot = jnp.arange(3)[None, None, None, None, :]
    code_all = slot * 9 + (k_band + 1) * 3 + width_slot
    matches = code_all[..., None] == jnp.arange(tile_flags.shape[2])
    picked = jnp.sum(jnp.where(matches, tile_flags[:, :, None, None, None, :], 0), axis=-1) > 0
    itself = (slot == 1) & (k_band == 0) & (width_slot == 1)
    time_valid = time_base + q_time + slot - 1 >= 0
    band_now = band_index + k_band
    band_valid = (band_now >= 0) & (band_now < band_total)
    col_now = q_width + width_slot - 1
    col_valid = (col_now >= 0) & (col_now < w_tiles)
    return (picked | itself) & time_valid & band_valid & col_valid


def token_allowed(tiles_ok, row_count):
    q_tiles, w_tiles = (tiles_ok.shape[0], tiles_ok.shape[1])
    tile_tokens = TF * row_count * TC
    grid = tiles_ok[:, :, None, :, None, :, None, :, None]
    full = jnp.broadcast_to(grid, (q_tiles, w_tiles, tile_tokens, 2, TF, 3, row_count, 3, TC))
    return full.reshape(q_tiles, w_tiles, tile_tokens, 2 * TF * 3 * row_count * 3 * TC)


def shards(queries, keys, values, tile_mask, sink_frame):
    frames, row_count, col_count, features = queries.shape
    head_count = H
    scaling = 1.0 / math.sqrt(HD)
    local_tiles = frames // TF
    width_tiles = col_count // TC
    tile_tokens = TF * row_count * TC
    token_count = frames * row_count * col_count
    key_vals = jnp.stack((keys, values))
    prior_keys = from_behind(key_vals, "tm", 1)
    joined = jnp.concatenate((prior_keys, key_vals), axis=1)
    window = with_halo(joined, (("height", 2),), row_count)
    q_tiled = queries.reshape(local_tiles, TF, row_count, width_tiles, TC, head_count, HD)
    q_tiled = jnp.transpose(q_tiled, (0, 3, 1, 2, 4, 5, 6)).reshape(
        local_tiles, width_tiles, tile_tokens, head_count, HD
    )
    q_flat = q_tiled.reshape(token_count, head_count, HD)
    tiles_ok = near_allowed(
        tile_mask[:, 0],
        lax.axis_index("tm") * local_tiles,
        lax.axis_index("height"),
        lax.axis_size("height"),
    )
    allowed = token_allowed(tiles_ok, row_count)
    group_size = math.gcd(head_count, 4)
    group_count = head_count // group_size

    def head_step(step_no, running):
        run_max, run_sum, summed = running
        offset = step_no * group_size
        q_part = lax.dynamic_slice_in_dim(q_tiled, offset, group_size, 3)
        win_part = lax.dynamic_slice_in_dim(window, offset * HD, group_size * HD, 4)
        padded = jnp.pad(win_part, ((0, 0), (0, 0), (0, 0), (TC, TC), (0, 0)))
        tiled = padded.reshape(
            2, local_tiles + 1, TF, 3 * row_count, col_count + 2 * TC, group_size * HD
        )
        paired = jnp.stack((tiled[:, :-1], tiled[:, 1:]), axis=2)
        shifted = jnp.stack(
            [
                paired[:, :, :, :, :, shift_no * TC : shift_no * TC + col_count]
                for shift_no in range(3)
            ],
            axis=5,
        )
        shifted = shifted.reshape(
            2, local_tiles, 2, TF, 3, row_count, 3, width_tiles, TC, group_size, HD
        )
        shifted = jnp.transpose(shifted, (0, 1, 7, 2, 3, 4, 5, 6, 8, 9, 10))
        shifted = shifted.reshape(2, local_tiles, width_tiles, -1, group_size, HD)
        scores = (
            jnp.einsum("tcqhd,tckhd->tchqk", q_part, shifted[0], preferred_element_type=jnp.float32)
            * scaling
        )
        scores = jnp.where(allowed[:, :, None], scores, masked_score)
        row_max = jnp.max(scores, axis=-1)
        weights = jnp.exp(scores - row_max[..., None]).astype(jnp.bfloat16)
        row_sum = jnp.sum(weights, axis=-1, dtype=jnp.float32)
        partial_out = jnp.einsum(
            "tchqk,tckhd->tcqhd", weights, shifted[1], preferred_element_type=jnp.float32
        )
        row_max = jnp.transpose(row_max, (2, 0, 1, 3)).reshape(group_size, token_count)
        row_sum = jnp.transpose(row_sum, (2, 0, 1, 3)).reshape(group_size, token_count)
        partial_out = partial_out.reshape(token_count, group_size, HD)
        run_max = lax.dynamic_update_slice_in_dim(run_max, row_max, offset, 0)
        run_sum = lax.dynamic_update_slice_in_dim(run_sum, row_sum, offset, 0)
        summed = lax.dynamic_update_slice_in_dim(summed, partial_out, offset, 1)
        return (run_max, run_sum, summed)

    window_init = (
        jnp.zeros((head_count, token_count), jnp.float32),
        jnp.zeros((head_count, token_count), jnp.float32),
        jnp.zeros((token_count, head_count, HD), jnp.float32),
    )
    win_max, win_sum, win_out = lax.fori_loop(0, group_count, head_step, window_init)
    sink_init = (
        jnp.full((head_count, token_count), masked_score, jnp.float32),
        jnp.zeros((head_count, token_count), jnp.float32),
        jnp.zeros((token_count, head_count, HD), jnp.float32),
    )
    owner_index = sink_frame[0] // frames
    local_frame = sink_frame[0] % frames
    sink_piece = lax.dynamic_slice_in_dim(key_vals, local_frame, 1, 1)[:, 0]
    sliced = from_root(sink_piece, "tm", owner_index)
    shard_rows = lax.all_gather(sliced, "height", axis=1, tiled=True)
    band_total = shard_rows.shape[1] // row_count

    def band_step(step_no, state):
        run_max, run_sum, summed = state
        block_rows = lax.dynamic_slice_in_dim(shard_rows, step_no * row_count, row_count, 1)
        key_block = block_rows[0].reshape(row_count * col_count, head_count, HD)
        val_block = block_rows[1].reshape(row_count * col_count, head_count, HD)
        scores = (
            jnp.einsum("qhd,khd->hqk", q_flat, key_block, preferred_element_type=jnp.float32)
            * scaling
        )
        row_max = jnp.max(scores, axis=-1)
        weights = jnp.exp(scores - row_max[..., None]).astype(jnp.bfloat16)
        row_sum = jnp.sum(weights, axis=-1, dtype=jnp.float32)
        added = jnp.einsum("hqk,khd->qhd", weights, val_block, preferred_element_type=jnp.float32)
        new_max = jnp.maximum(run_max, row_max)
        keep_old = jnp.exp(run_max - new_max)
        factor = jnp.exp(row_max - new_max)
        run_sum = run_sum * keep_old + row_sum * factor
        summed = summed * keep_old.T[..., None] + added * factor.T[..., None]
        return (new_max, run_sum, summed)

    sink_max, sink_sum, sink_out = lax.fori_loop(0, band_total, band_step, sink_init)
    top_score = jnp.maximum(win_max, sink_max)
    win_factor = jnp.exp(win_max - top_score)
    sink_factor = jnp.exp(sink_max - top_score)
    denominator = win_factor * win_sum + sink_factor * sink_sum
    numerator = win_out * win_factor.T[..., None] + sink_out * sink_factor.T[..., None]
    result = (numerator / denominator.T[..., None]).astype(jnp.bfloat16)
    result = result.reshape(local_tiles, width_tiles, TF, row_count, TC, features)
    result = jnp.transpose(result, (0, 2, 3, 1, 4, 5))
    return result.reshape(frames, row_count, col_count, features)


def solution(mesh):
    return jax.shard_map(
        shards,
        mesh=mesh,
        in_specs=(
            P("tm", "height", None, None),
            P("tm", "height", None, None),
            P("tm", "height", None, None),
            P("tm", "height", None, None),
            P(),
        ),
        out_specs=P("tm", "height", None, None),
        check_vma=False,
    )
```

profile of v0, /device:TPU:1, one launch (start us, length us, event | category | flops | bytes accessed | tf_op | source)
XLA Modules:
  0.0 239.6 jit_solution(7108686175418753605)
XLA Ops:
  6.5 2.6 %pad_maximum_fusion.2 = bf16[2,4,2,16,2560]{4,3,2,0,1:T(8,128)(2,1)} fusion(bf16[1,4,2,16,2560]{4,3,2,0,1:T(8,128)(2,1)} %bitcast.136, bf16[1,4,2,16,2560]{4,3,2,0,1:T(8,128)(2,1)} %bitcast.132), kind=kLoop, calls=%fused_computation.45 | loop fusion | flops 655360 | bytes 2621440 | tf_op jit(solution)/shard_map/stack | solution.py:78
  9.2 4.1 %collective-permute-start = (bf16[2,4,2,16,2560]{4,3,2,0,1:T(8,128)(2,1)}, bf16[2,4,2,16,2560]{4,3,2,0,1:T(8,128)(2,1)S(1)}, u32[]{:S(2)}, u32[]{:S(2)}) collective-permute-start(bf16[2,4,2,16,2560]{4,3,2,0,1:T(8,128)(2,1)} %pad_maximum_fusion.2), channel_id=1, source_target_pairs={{0,8},{8,16},{16,24},{1,9},{9,17},{17,25},{2,10},{10,18},{18,26},{... | collective-permute-start | bytes 3932168 | tf_op jit(solution)/shard_map/ppermute | solution.py:17
  14.0 27.0 %collective-permute-done = bf16[2,4,2,16,2560]{4,3,2,0,1:T(8,128)(2,1)S(1)} collective-permute-done((bf16[2,4,2,16,2560]{4,3,2,0,1:T(8,128)(2,1)}, bf16[2,4,2,16,2560]{4,3,2,0,1:T(8,128)(2,1)S(1)}, u32[]{:S(2)}, u32[]{:S(2)}) %collective-permute-start) | collective-permute-done | bytes 1310752 | tf_op jit(solution)/shard_map/ppermute | solution.py:17
  41.0 1.8 maximum_maximum_fusion
  42.7 4.5 %collective-permute-start.1 = (bf16[2,8,2,16,2560]{4,3,2,0,1:T(8,128)(2,1)}, bf16[2,8,2,16,2560]{4,3,2,0,1:T(8,128)(2,1)}, u32[]{:S(2)}, u32[]{:S(2)}) collective-permute-start(bf16[2,8,2,16,2560]{4,3,2,0,1:T(8,128)(2,1)} %maximum_maximum_fusion), channel_id=1, source_target_pairs={{0,1},{1,2},{2,3},{3,4},{4,5},{5,6},{6,7},{8,9},{9,10},{10,11},{11... | collective-permute-start | bytes 7864328 | tf_op jit(solution)/shard_map/ppermute | solution.py:28
  47.2 1.9 collective-permute-start.2
  51.1 1.2 copy_bitcast_fusion.1
  53.2 33.5 %all-reduce.3.cloned.1.call-done = bf16[2,2,16,2560]{3,2,1,0:T(8,128)(2,1)} async-done(((bf16[2,2,16,2560]{3,2,1,0:T(8,128)(2,1)}), bf16[2,2,16,2560]{3,2,1,0:T(8,128)(2,1)}) %all-reduce.3.cloned.1.call-update) | async-done | bytes 327696 | tf_op jit(solution)/shard_map/psum | solution.py:39
  86.7 22.7 %collective-permute-done.2 = bf16[2,8,2,16,2560]{4,3,2,0,1:T(8,128)(2,1)} collective-permute-done((bf16[2,8,2,16,2560]{4,3,2,0,1:T(8,128)(2,1)}, bf16[2,8,2,16,2560]{4,3,2,0,1:T(8,128)(2,1)}, u32[]{:S(2)}, u32[]{:S(2)}) %collective-permute-start.2) | collective-permute-done | bytes 2621472 | tf_op jit(solution)/shard_map/ppermute | solution.py:30
  109.4 6.5 %pad_maximum_fusion.1 = bf16[2,8,6,16,2560]{4,3,2,0,1:T(8,128)(2,1)} fusion(bf16[2,8,2,16,2560]{4,3,2,0,1:T(8,128)(2,1)} %collective-permute-done.2, bf16[1,4,2,16,2560]{4,3,2,0,1:T(8,128)(2,1)S(1)} %bitcast.139, bf16[1,4,2,16,2560]{4,3,2,0,1:T(8,128)(2,1)S(1)} %bitcast.135, bf16[2,4,2,16,2560]{4,3,2,0,1:T(8,128)(2,1)S(1)} %collective-permute-done, ...), kind=kLoop, calls=%fused_computation.42 | loop fusion | flops 15728640 | bytes 15728640 | tf_op jit(solution)/shard_map/concatenate | solution.py:26
  115.9 1.2 broadcast.334.clone.1
  117.1 74.7 %while.38 = (s32[]{:T(128)}, f32[20,128]{1,0:T(8,128)S(1)}, f32[20,128]{1,0:T(8,128)S(1)}, f32[128,20,128]{0,2,1:T(8,128)}, bf16[1,2,64,20,128]{4,2,3,1,0:T(8,12...) while((s32[]{:T(128)}, f32[20,128]{1,0:T(8,128)S(1)}, ...), condition=%wide.region_4.5_spmd.clone, body=%wide.region_1.4_spmd.clone.sunk | while | flops 321453056 | bytes 86737208 | solution.py:143
  117.1 1.5 constant_dynamic-slice_fusion.5
  121.1 2.5 %fusion.46 = (bf16[1,1,2,2,4,3,2,3,8,4,128]{10,8,9,2,7,6,5,4,3,1,0:T(8,128)(2,1)}, bf16[1,1,2,2,4,3,2,3,8,4,128]{10,8,9,2,7,6,5,4,3,1,0:T(8,128)(2,1)S(1)}) fusion(bf16[2,1,2,2,4,3,2,3,8,4,128]{10,8,9,2,7,6,5,4,3,1,0:T(8,128)(2,1)S(1)} %maximum_bitcast_fusion.2), kind=kLoop, calls=%fused_computation.76.clone.1 | loop fusion | bytes 9437184 | tf_op jit(solution)/shard_map/while/body/eval_jaxpr/slice | solution.py:128
  123.6 2.0 copy.127
  126.2 3.0 %fusion.47 = (f32[2,4,64]{2,1,0:T(4,128)S(1)}, f32[2,4,64,1152]{3,2,1,0:T(8,128)S(1)}) fusion(bf16[2,1152,4,128]{3,1,2,0:T(8,128)(2,1)} %bitcast.124, bf16[1,2,64,20,128]{4,2,3,1,0:T(8,128)(2,1)} %get-tuple-element.616, s32[]{:T(128)S(6)} %select_n.100, pred[2,64,1152]{2,1,0:T(8,128)(4,1)S(1)} %copy.128), kind=kOutput, calls=%fused_computation.77.clone.1 | convolution fusion | flops 152763904 | bytes 4999172 | tf_op jit(solution)/shard_map/while/body/eval_jaxpr/tcqhd,tckhd->tchqk/dot_general | solution.py:120
  132.1 1.5 constant_dynamic-slice_fusion.5
  136.0 2.5 %fusion.46 = (bf16[1,1,2,2,4,3,2,3,8,4,128]{10,8,9,2,7,6,5,4,3,1,0:T(8,128)(2,1)}, bf16[1,1,2,2,4,3,2,3,8,4,128]{10,8,9,2,7,6,5,4,3,1,0:T(8,128)(2,1)S(1)}) fusion(bf16[2,1,2,2,4,3,2,3,8,4,128]{10,8,9,2,7,6,5,4,3,1,0:T(8,128)(2,1)S(1)} %maximum_bitcast_fusion.2), kind=kLoop, calls=%fused_computation.76.clone.1 | loop fusion | bytes 9437184 | tf_op jit(solution)/shard_map/while/body/eval_jaxpr/slice | solution.py:128
  138.5 2.0 copy.127
  141.1 3.0 %fusion.47 = (f32[2,4,64]{2,1,0:T(4,128)S(1)}, f32[2,4,64,1152]{3,2,1,0:T(8,128)S(1)}) fusion(bf16[2,1152,4,128]{3,1,2,0:T(8,128)(2,1)} %bitcast.124, bf16[1,2,64,20,128]{4,2,3,1,0:T(8,128)(2,1)} %get-tuple-element.616, s32[]{:T(128)S(6)} %select_n.100, pred[2,64,1152]{2,1,0:T(8,128)(4,1)S(1)} %copy.128), kind=kOutput, calls=%fused_computation.77.clone.1 | convolution fusion | flops 152763904 | bytes 4999172 | tf_op jit(solution)/shard_map/while/body/eval_jaxpr/tcqhd,tckhd->tchqk/dot_general | solution.py:120
  147.0 1.5 constant_dynamic-slice_fusion.5
  150.9 2.5 %fusion.46 = (bf16[1,1,2,2,4,3,2,3,8,4,128]{10,8,9,2,7,6,5,4,3,1,0:T(8,128)(2,1)}, bf16[1,1,2,2,4,3,2,3,8,4,128]{10,8,9,2,7,6,5,4,3,1,0:T(8,128)(2,1)S(1)}) fusion(bf16[2,1,2,2,4,3,2,3,8,4,128]{10,8,9,2,7,6,5,4,3,1,0:T(8,128)(2,1)S(1)} %maximum_bitcast_fusion.2), kind=kLoop, calls=%fused_computation.76.clone.1 | loop fusion | bytes 9437184 | tf_op jit(solution)/shard_map/while/body/eval_jaxpr/slice | solution.py:128
  153.5 2.0 copy.127
  156.0 3.0 %fusion.47 = (f32[2,4,64]{2,1,0:T(4,128)S(1)}, f32[2,4,64,1152]{3,2,1,0:T(8,128)S(1)}) fusion(bf16[2,1152,4,128]{3,1,2,0:T(8,128)(2,1)} %bitcast.124, bf16[1,2,64,20,128]{4,2,3,1,0:T(8,128)(2,1)} %get-tuple-element.616, s32[]{:T(128)S(6)} %select_n.100, pred[2,64,1152]{2,1,0:T(8,128)(4,1)S(1)} %copy.128), kind=kOutput, calls=%fused_computation.77.clone.1 | convolution fusion | flops 152763904 | bytes 4999172 | tf_op jit(solution)/shard_map/while/body/eval_jaxpr/tcqhd,tckhd->tchqk/dot_general | solution.py:120
  161.9 1.5 constant_dynamic-slice_fusion.5
  165.9 2.5 %fusion.46 = (bf16[1,1,2,2,4,3,2,3,8,4,128]{10,8,9,2,7,6,5,4,3,1,0:T(8,128)(2,1)}, bf16[1,1,2,2,4,3,2,3,8,4,128]{10,8,9,2,7,6,5,4,3,1,0:T(8,128)(2,1)S(1)}) fusion(bf16[2,1,2,2,4,3,2,3,8,4,128]{10,8,9,2,7,6,5,4,3,1,0:T(8,128)(2,1)S(1)} %maximum_bitcast_fusion.2), kind=kLoop, calls=%fused_computation.76.clone.1 | loop fusion | bytes 9437184 | tf_op jit(solution)/shard_map/while/body/eval_jaxpr/slice | solution.py:128
  168.4 2.0 copy.127
  171.0 3.0 %fusion.47 = (f32[2,4,64]{2,1,0:T(4,128)S(1)}, f32[2,4,64,1152]{3,2,1,0:T(8,128)S(1)}) fusion(bf16[2,1152,4,128]{3,1,2,0:T(8,128)(2,1)} %bitcast.124, bf16[1,2,64,20,128]{4,2,3,1,0:T(8,128)(2,1)} %get-tuple-element.616, s32[]{:T(128)S(6)} %select_n.100, pred[2,64,1152]{2,1,0:T(8,128)(4,1)S(1)} %copy.128), kind=kOutput, calls=%fused_computation.77.clone.1 | convolution fusion | flops 152763904 | bytes 4999172 | tf_op jit(solution)/shard_map/while/body/eval_jaxpr/tcqhd,tckhd->tchqk/dot_general | solution.py:120
  176.9 1.5 constant_dynamic-slice_fusion.5
  180.8 2.5 %fusion.46 = (bf16[1,1,2,2,4,3,2,3,8,4,128]{10,8,9,2,7,6,5,4,3,1,0:T(8,128)(2,1)}, bf16[1,1,2,2,4,3,2,3,8,4,128]{10,8,9,2,7,6,5,4,3,1,0:T(8,128)(2,1)S(1)}) fusion(bf16[2,1,2,2,4,3,2,3,8,4,128]{10,8,9,2,7,6,5,4,3,1,0:T(8,128)(2,1)S(1)} %maximum_bitcast_fusion.2), kind=kLoop, calls=%fused_computation.76.clone.1 | loop fusion | bytes 9437184 | tf_op jit(solution)/shard_map/while/body/eval_jaxpr/slice | solution.py:128
  183.3 2.0 copy.127
  185.9 3.0 %fusion.47 = (f32[2,4,64]{2,1,0:T(4,128)S(1)}, f32[2,4,64,1152]{3,2,1,0:T(8,128)S(1)}) fusion(bf16[2,1152,4,128]{3,1,2,0:T(8,128)(2,1)} %bitcast.124, bf16[1,2,64,20,128]{4,2,3,1,0:T(8,128)(2,1)} %get-tuple-element.616, s32[]{:T(128)S(6)} %select_n.100, pred[2,64,1152]{2,1,0:T(8,128)(4,1)S(1)} %copy.128), kind=kOutput, calls=%fused_computation.77.clone.1 | convolution fusion | flops 152763904 | bytes 4999172 | tf_op jit(solution)/shard_map/while/body/eval_jaxpr/tcqhd,tckhd->tchqk/dot_general | solution.py:120
  191.8 37.5 %while.39 = (s32[]{:T(128)}, f32[20,128]{1,0:T(8,128)S(1)}, f32[20,128]{1,0:T(8,128)S(1)}, f32[128,20,128]{0,2,1:T(8,128)}, bf16[2,16,16,2560]{3,2,1,0:T(8,128)(...) while((s32[]{:T(128)}, f32[20,128]{1,0:T(8,128)S(1)}, ...), condition=%wide.region_9.10_spmd.clone, body=%wide.region_6.9_spmd.clone.sunk | while | flops 43929608 | bytes 16578803 | solution.py:176
  191.8 1.2 constant_dynamic-slice_fusion.6
  193.1 1.5 fusion.50
  196.6 1.1 constant_dynamic-slice_fusion.6
  197.8 1.5 fusion.50
  201.2 1.1 constant_dynamic-slice_fusion.6
  202.5 1.5 fusion.50
  205.9 1.1 constant_dynamic-slice_fusion.6
  207.2 1.5 fusion.50
  210.6 1.1 constant_dynamic-slice_fusion.6
  211.8 1.5 fusion.50
  215.3 1.1 constant_dynamic-slice_fusion.6
  216.5 1.5 fusion.50
  221.2 1.5 fusion.50
  225.9 1.5 fusion.50
  229.3 1.7 divide_convert_fusion
  (249 shorter events, 50.8 us)
Async XLA Ops:
  6.5 44.5 %copy-start = (bf16[4,2,16,2560]{3,2,1,0:T(8,128)(2,1)S(1)}, bf16[4,2,16,2560]{3,2,1,0:T(8,128)(2,1)}, u32[]{:S(2)}) copy-start(bf16[4,2,16,2560]{3,2,1,0:T(8,128)(2,1)} %param.9) | copy-start | bytes 1966084
  6.5 34.4 %copy-start.5 = (bf16[4,2,16,2560]{3,2,1,0:T(8,128)(2,1)S(1)}, bf16[4,2,16,2560]{3,2,1,0:T(8,128)(2,1)}, u32[]{:S(2)}) copy-start(bf16[4,2,16,2560]{3,2,1,0:T(8,128)(2,1)} %param.10) | copy-start | bytes 1966084
  6.5 34.4 %copy-start.6 = (bf16[4,2,16,2560]{3,2,1,0:T(8,128)(2,1)S(1)}, bf16[4,2,16,2560]{3,2,1,0:T(8,128)(2,1)}, u32[]{:S(2)}) copy-start(bf16[4,2,16,2560]{3,2,1,0:T(8,128)(2,1)} %param.11) | copy-start | bytes 1966084
  6.5 80.1 %all-reduce.3.cloned.1.call-start = ((), (), s32[]{:S(2)}) async-start(), calls=%async_computation | async-start | bytes 655360 | tf_op jit(solution)/shard_map/psum | solution.py:39
  9.2 31.8 %collective-permute-start = (bf16[2,4,2,16,2560]{4,3,2,0,1:T(8,128)(2,1)}, bf16[2,4,2,16,2560]{4,3,2,0,1:T(8,128)(2,1)S(1)}, u32[]{:S(2)}, u32[]{:S(2)}) collective-permute-start(bf16[2,4,2,16,2560]{4,3,2,0,1:T(8,128)(2,1)} %pad_maximum_fusion.2), channel_id=1, source_target_pairs={{0,8},{8,16},{16,24},{1,9},{9,17},{17,25},{2,10},{10,18},{18,26},{... | collective-permute-start | bytes 3932168 | tf_op jit(solution)/shard_map/ppermute | solution.py:17
  14.0 36.3 %copy-start.8 = (s32[1,1,2,18]{3,2,1,0:T(2,128)S(1)}, s32[1,1,2,18]{3,2,1,0:T(2,128)}, u32[]{:S(2)}) copy-start(s32[1,1,2,18]{3,2,1,0:T(2,128)} %param.12) | copy-start | bytes 436
  42.7 44.0 %collective-permute-start.1 = (bf16[2,8,2,16,2560]{4,3,2,0,1:T(8,128)(2,1)}, bf16[2,8,2,16,2560]{4,3,2,0,1:T(8,128)(2,1)}, u32[]{:S(2)}, u32[]{:S(2)}) collective-permute-start(bf16[2,8,2,16,2560]{4,3,2,0,1:T(8,128)(2,1)} %maximum_maximum_fusion), channel_id=1, source_target_pairs={{0,1},{1,2},{2,3},{3,4},{4,5},{5,6},{6,7},{8,9},{9,10},{10,11},{11... | collective-permute-start | bytes 7864328 | tf_op jit(solution)/shard_map/ppermute | solution.py:28
  47.2 62.1 %collective-permute-start.2 = (bf16[2,8,2,16,2560]{4,3,2,0,1:T(8,128)(2,1)}, bf16[2,8,2,16,2560]{4,3,2,0,1:T(8,128)(2,1)}, u32[]{:S(2)}, u32[]{:S(2)}) collective-permute-start(bf16[2,8,2,16,2560]{4,3,2,0,1:T(8,128)(2,1)} %maximum_maximum_fusion), channel_id=1, source_target_pairs={{1,0},{2,1},{3,2},{4,3},{5,4},{6,5},{7,6},{9,8},{10,9},{11,10},{12... | collective-permute-start | bytes 7864328 | tf_op jit(solution)/shard_map/ppermute | solution.py:30
  50.0 141.8 %all-gather.2.cloned.1.call-start = ((), (), s32[]{:S(2)}) async-start(), calls=%async_computation.1 | async-start | bytes 2949120 | tf_op jit(solution)/shard_map/all_gather | solution.py:153
  126.1 3.0 %copy-start.2 = (bf16[1,1,2,2,4,3,2,3,8,4,128]{10,8,9,2,7,6,5,4,3,1,0:T(8,128)(2,1)S(1)}, bf16[1,1,2,2,4,3,2,3,8,4,128]{10,8,9,2,7,6,5,4,3,1,0:T(8,128)(2,1)}, u32[]{:S(2)}) copy-start(bf16[1,1,2,2,4,3,2,3,8,4,128]{10,8,9,2,7,6,5,4,3,1,0:T(8,128)(2,1)} %get-tuple-element.536) | copy-start | bytes 7077892 | tf_op jit(solution)/shard_map/while
  141.1 3.0 %copy-start.2 = (bf16[1,1,2,2,4,3,2,3,8,4,128]{10,8,9,2,7,6,5,4,3,1,0:T(8,128)(2,1)S(1)}, bf16[1,1,2,2,4,3,2,3,8,4,128]{10,8,9,2,7,6,5,4,3,1,0:T(8,128)(2,1)}, u32[]{:S(2)}) copy-start(bf16[1,1,2,2,4,3,2,3,8,4,128]{10,8,9,2,7,6,5,4,3,1,0:T(8,128)(2,1)} %get-tuple-element.536) | copy-start | bytes 7077892 | tf_op jit(solution)/shard_map/while
  156.0 3.0 %copy-start.2 = (bf16[1,1,2,2,4,3,2,3,8,4,128]{10,8,9,2,7,6,5,4,3,1,0:T(8,128)(2,1)S(1)}, bf16[1,1,2,2,4,3,2,3,8,4,128]{10,8,9,2,7,6,5,4,3,1,0:T(8,128)(2,1)}, u32[]{:S(2)}) copy-start(bf16[1,1,2,2,4,3,2,3,8,4,128]{10,8,9,2,7,6,5,4,3,1,0:T(8,128)(2,1)} %get-tuple-element.536) | copy-start | bytes 7077892 | tf_op jit(solution)/shard_map/while
  171.0 3.0 %copy-start.2 = (bf16[1,1,2,2,4,3,2,3,8,4,128]{10,8,9,2,7,6,5,4,3,1,0:T(8,128)(2,1)S(1)}, bf16[1,1,2,2,4,3,2,3,8,4,128]{10,8,9,2,7,6,5,4,3,1,0:T(8,128)(2,1)}, u32[]{:S(2)}) copy-start(bf16[1,1,2,2,4,3,2,3,8,4,128]{10,8,9,2,7,6,5,4,3,1,0:T(8,128)(2,1)} %get-tuple-element.536) | copy-start | bytes 7077892 | tf_op jit(solution)/shard_map/while
  185.9 3.0 %copy-start.2 = (bf16[1,1,2,2,4,3,2,3,8,4,128]{10,8,9,2,7,6,5,4,3,1,0:T(8,128)(2,1)S(1)}, bf16[1,1,2,2,4,3,2,3,8,4,128]{10,8,9,2,7,6,5,4,3,1,0:T(8,128)(2,1)}, u32[]{:S(2)}) copy-start(bf16[1,1,2,2,4,3,2,3,8,4,128]{10,8,9,2,7,6,5,4,3,1,0:T(8,128)(2,1)} %get-tuple-element.536) | copy-start | bytes 7077892 | tf_op jit(solution)/shard_map/while
  191.8 37.5 %copy-start.7 = (f32[128,20,128]{0,2,1:T(8,128)S(1)}, f32[128,20,128]{0,2,1:T(8,128)}, u32[]{:S(2)}) copy-start(f32[128,20,128]{0,2,1:T(8,128)} %get-tuple-element.295) | copy-start | bytes 3932164
  191.8 3.1 %copy-start.3 = (f32[128,20,128]{0,2,1:T(8,128)S(1)}, f32[128,20,128]{0,2,1:T(8,128)}, u32[]{:S(2)}) copy-start(f32[128,20,128]{0,2,1:T(8,128)} %get-tuple-element.565) | copy-start | bytes 3932164 | tf_op jit(solution)/shard_map/while
  195.5 1.1 copy-start.4
  196.6 3.0 %copy-start.3 = (f32[128,20,128]{0,2,1:T(8,128)S(1)}, f32[128,20,128]{0,2,1:T(8,128)}, u32[]{:S(2)}) copy-start(f32[128,20,128]{0,2,1:T(8,128)} %get-tuple-element.565) | copy-start | bytes 3932164 | tf_op jit(solution)/shard_map/while
  200.2 1.1 copy-start.4
  201.2 3.0 %copy-start.3 = (f32[128,20,128]{0,2,1:T(8,128)S(1)}, f32[128,20,128]{0,2,1:T(8,128)}, u32[]{:S(2)}) copy-start(f32[128,20,128]{0,2,1:T(8,128)} %get-tuple-element.565) | copy-start | bytes 3932164 | tf_op jit(solution)/shard_map/while
  204.8 1.1 copy-start.4
  205.9 3.0 %copy-start.3 = (f32[128,20,128]{0,2,1:T(8,128)S(1)}, f32[128,20,128]{0,2,1:T(8,128)}, u32[]{:S(2)}) copy-start(f32[128,20,128]{0,2,1:T(8,128)} %get-tuple-element.565) | copy-start | bytes 3932164 | tf_op jit(solution)/shard_map/while
  209.5 1.1 copy-start.4
  210.6 3.0 %copy-start.3 = (f32[128,20,128]{0,2,1:T(8,128)S(1)}, f32[128,20,128]{0,2,1:T(8,128)}, u32[]{:S(2)}) copy-start(f32[128,20,128]{0,2,1:T(8,128)} %get-tuple-element.565) | copy-start | bytes 3932164 | tf_op jit(solution)/shard_map/while
  214.2 1.1 copy-start.4
  215.3 3.0 %copy-start.3 = (f32[128,20,128]{0,2,1:T(8,128)S(1)}, f32[128,20,128]{0,2,1:T(8,128)}, u32[]{:S(2)}) copy-start(f32[128,20,128]{0,2,1:T(8,128)} %get-tuple-element.565) | copy-start | bytes 3932164 | tf_op jit(solution)/shard_map/while
  218.9 1.1 copy-start.4
  219.9 3.0 %copy-start.3 = (f32[128,20,128]{0,2,1:T(8,128)S(1)}, f32[128,20,128]{0,2,1:T(8,128)}, u32[]{:S(2)}) copy-start(f32[128,20,128]{0,2,1:T(8,128)} %get-tuple-element.565) | copy-start | bytes 3932164 | tf_op jit(solution)/shard_map/while
  223.5 1.1 copy-start.4
  224.6 3.0 %copy-start.3 = (f32[128,20,128]{0,2,1:T(8,128)S(1)}, f32[128,20,128]{0,2,1:T(8,128)}, u32[]{:S(2)}) copy-start(f32[128,20,128]{0,2,1:T(8,128)} %get-tuple-element.565) | copy-start | bytes 3932164 | tf_op jit(solution)/shard_map/while
  228.2 1.1 copy-start.4
  229.3 3.4 %copy-start.1 = (bf16[4,2,16,2560]{3,2,1,0:T(8,128)(2,1)S(1)}, bf16[4,2,16,2560]{3,2,1,0:T(8,128)(2,1)}, u32[]{:S(2)}) copy-start(bf16[4,2,16,2560]{3,2,1,0:T(8,128)(2,1)} %param.9) | copy-start | bytes 1966084
Sparse Core Ops, SparseCore 0:
  50.1 36.5 all-reduce.2
  88.5 35.1 all-gather.1
where the time goes:
time: 240 us
  waiting for transfers between devices  83.2 us (35%)
  local copies, waits for them, and re-layouts  72.7 us (30%)
  matrix products  35 us (15%)
  other arithmetic  22.5 us (9%)
  between operations  14.2 us (6%)
  starting transfers between devices  10.6 us (4%)
    psum x1, waiting for transfers between devices, from_root(): return lax.psum(jnp.where(mine, x, jnp.zeros_like(x)), axis)  33.5 us
    ppermute x1, waiting for transfers between devices, from_behind(): lax.ppermute(value, axis, [(source, source + steps) for source in range(f...  27 us
    ppermute x1, waiting for transfers between devices, with_halo(): lax.ppermute(head, axis, [((i + 1) % count, i) for i in range(ends)])  22.7 us
    slice x10, local copies, waits for them, and re-layouts, head_step(): shifted[1]  15.8 us
    dot_general x5, matrix products, head_step(): jnp.einsum('tcqhd,tckhd->tchqk', q_part, shifted[0], preferred_element_ty...  14.9 us
    dot_general x8, matrix products, band_step(): jnp.einsum('qhd,khd->hqk', q_flat, key_block, preferred_element_type=jnp....  12.4 us
    slice x5, local copies, waits for them, and re-layouts, head_step(): shifted[0]  10 us
    slice x8, local copies, waits for them, and re-layouts, band_step(): val_block = block_rows[1].reshape(row_count * col_count, head_count, HD)  9.01 us
  transfers between devices with their start and end apart: 5, of which 3 were waited for; matrix products, arithmetic and copies ran while one was open for 36% of the time, Pallas kernels for 0%

commit v1 on v0

--- a/solution.py
+++ b/solution.py
@@ -36,7 +36,8 @@
 
 def from_root(x, axis, root):
     mine = lax.axis_index(axis) == root
-    return lax.psum(jnp.where(mine, x, jnp.zeros_like(x)), axis)
+    cells_read = lambda panel, mesh_name: jnp.sum(jax.lax.all_gather(panel, axis_name=mesh_name), 0)
+    return cells_read(jnp.where(mine, x, jnp.zeros_like(x)), axis)
 
 
 def near_allowed(tile_flags, time_base, band_index, band_total):

time: 240 us -> 267 us (1.11)
  waiting for transfers between devices: 83.2 us -> 105 us
    psum x1 -> x0, waiting for transfers between devices: 33.5 us -> none  [from_root(): return lax.psum(jnp.where(mine, x, jnp.zeros_like(x)), axis)]
    ppermute x1, waiting for transfers between devices: 0.01 us -> 25 us  [with_halo(): lax.ppermute(tail, axis, [(i, (i + 1) % count) for i in range(ends)])]
    ppermute x1, waiting for transfers between devices: 27 us -> 43.2 us  [from_behind(): lax.ppermute(value, axis, [(source, source + steps) for source in range(f...]
    ppermute x1, waiting for transfers between devices: 22.7 us -> 36.8 us  [with_halo(): lax.ppermute(head, axis, [((i + 1) % count, i) for i in range(ends)])]
    dynamic_slice x10 -> x5, local copies, waits for them, and re-layouts: 8.49 us -> 7.66 us  [head_step(): win_part = lax.dynamic_slice_in_dim(window, offset * HD, group_size * HD, 4)]
  transfers between devices with their start and end apart: 5 -> 5, of which waited for: 3 -> 3; matrix products, arithmetic and copies ran while one was open for 36% -> 33% of each run, Pallas kernels for 0% -> 0%
where the time goes in v1:
time: 267 us; the launch traced here: 265 us
  waiting for transfers between devices  105 us (39%)
  local copies, waits for them, and re-layouts  71.9 us (27%)
  matrix products  35 us (13%)
  other arithmetic  24.6 us (9%)
  between operations  14.3 us (5%)
  starting transfers between devices  12.6 us (5%)
    ppermute x1, waiting for transfers between devices, from_behind(): lax.ppermute(value, axis, [(source, source + steps) for source in range(f...  43.2 us
    ppermute x1, waiting for transfers between devices, with_halo(): lax.ppermute(head, axis, [((i + 1) % count, i) for i in range(ends)])  36.8 us
    ppermute x1, waiting for transfers between devices, with_halo(): lax.ppermute(tail, axis, [(i, (i + 1) % count) for i in range(ends)])  25 us
    slice x10, local copies, waits for them, and re-layouts, head_step(): shifted[1]  15.8 us
    dot_general x5, matrix products, head_step(): jnp.einsum('tcqhd,tckhd->tchqk', q_part, shifted[0], preferred_element_ty...  14.9 us
    dot_general x8, matrix products, band_step(): jnp.einsum('qhd,khd->hqk', q_flat, key_block, preferred_element_type=jnp....  12.4 us
    slice x5, local copies, waits for them, and re-layouts, head_step(): shifted[0]  10 us
    slice x8, local copies, waits for them, and re-layouts, band_step(): val_block = block_rows[1].reshape(row_count * col_count, head_count, HD)  9.01 us
  transfers between devices with their start and end apart: 5, of which 3 were waited for; matrix products, arithmetic and copies ran while one was open for 33% of the time, Pallas kernels for 0%

profile of v1, /device:TPU:1, one launch (start us, length us, event | category | flops | bytes accessed | tf_op | source)
XLA Modules:
  0.0 264.7 jit_solution(10323690618011730060)
XLA Ops:
  6.5 2.6 pad_maximum_fusion.2
  9.2 4.1 %collective-permute-start = (bf16[2,4,2,16,2560]{4,3,2,1,0:T(8,128)(2,1)}, bf16[2,4,2,16,2560]{4,3,2,1,0:T(8,128)(2,1)S(1)}, u32[]{:S(2)}, u32[]{:S(2)}) collective-permute-start(bf16[2,4,2,16,2560]{4,3,2,1,0:T(8,128)(2,1)} %pad_maximum_fusion.2), channel_id=1, source_target_pairs={{0,8},{8,16},{16,24},{1,9},{9,17},{17,25},{2,10},{10,18},{18,26},{... | collective-permute-start | bytes 3932168 | tf_op jit(solution)/shard_map/ppermute | solution.py:17
  14.8 43.2 %collective-permute-done = bf16[2,4,2,16,2560]{4,3,2,1,0:T(8,128)(2,1)S(1)} collective-permute-done((bf16[2,4,2,16,2560]{4,3,2,1,0:T(8,128)(2,1)}, bf16[2,4,2,16,2560]{4,3,2,1,0:T(8,128)(2,1)S(1)}, u32[]{:S(2)}, u32[]{:S(2)}) %collective-permute-start) | collective-permute-done | bytes 1310752 | tf_op jit(solution)/shard_map/ppermute | solution.py:17
  58.1 1.8 maximum_maximum_fusion
  59.8 6.6 %collective-permute-start.1 = (bf16[2,8,2,16,2560]{4,3,2,1,0:T(8,128)(2,1)}, bf16[2,8,2,16,2560]{4,3,2,1,0:T(8,128)(2,1)}, u32[]{:S(2)}, u32[]{:S(2)}) collective-permute-start(bf16[2,8,2,16,2560]{4,3,2,1,0:T(8,128)(2,1)} %maximum_maximum_fusion), channel_id=1, source_target_pairs={{0,1},{1,2},{2,3},{3,4},{4,5},{5,6},{6,7},{8,9},{9,10},{10,11},{11... | collective-permute-start | bytes 7864328 | tf_op jit(solution)/shard_map/ppermute | solution.py:28
  66.4 1.9 collective-permute-start.2
  69.4 1.2 copy_bitcast_fusion.1
  71.5 2.3 bitcast_reduce_fusion
  73.8 25.0 %collective-permute-done.1 = bf16[2,8,2,16,2560]{4,3,2,1,0:T(8,128)(2,1)} collective-permute-done((bf16[2,8,2,16,2560]{4,3,2,1,0:T(8,128)(2,1)}, bf16[2,8,2,16,2560]{4,3,2,1,0:T(8,128)(2,1)}, u32[]{:S(2)}, u32[]{:S(2)}) %collective-permute-start.1) | collective-permute-done | bytes 2621472 | tf_op jit(solution)/shard_map/ppermute | solution.py:28
  98.8 36.8 %collective-permute-done.2 = bf16[2,8,2,16,2560]{4,3,2,1,0:T(8,128)(2,1)} collective-permute-done((bf16[2,8,2,16,2560]{4,3,2,1,0:T(8,128)(2,1)}, bf16[2,8,2,16,2560]{4,3,2,1,0:T(8,128)(2,1)}, u32[]{:S(2)}, u32[]{:S(2)}) %collective-permute-start.2) | collective-permute-done | bytes 2621472 | tf_op jit(solution)/shard_map/ppermute | solution.py:30
  135.6 6.3 %pad_maximum_fusion.1 = bf16[2,8,6,16,2560]{4,3,2,1,0:T(8,128)(2,1)} fusion(bf16[2,8,2,16,2560]{4,3,2,1,0:T(8,128)(2,1)} %collective-permute-done.2, bf16[1,4,2,16,2560]{4,3,2,1,0:T(8,128)(2,1)S(1)} %bitcast.140, bf16[1,4,2,16,2560]{4,3,2,1,0:T(8,128)(2,1)S(1)} %bitcast.136, bf16[2,4,2,16,2560]{4,3,2,1,0:T(8,128)(2,1)S(1)} %collective-permute-done, ...), kind=kLoop, calls=%fused_computation.42 | loop fusion | flops 15728640 | bytes 15728640 | tf_op jit(solution)/shard_map/concatenate | solution.py:26
  141.9 1.2 broadcast.348.clone.1
  143.1 73.8 %while.38 = (s32[]{:T(128)}, f32[20,128]{1,0:T(8,128)S(1)}, f32[20,128]{1,0:T(8,128)S(1)}, f32[128,20,128]{0,2,1:T(8,128)}, bf16[1,2,64,20,128]{4,2,3,1,0:T(8,12...) while((s32[]{:T(128)}, f32[20,128]{1,0:T(8,128)S(1)}, ...), condition=%wide.region_4.5_spmd.clone, body=%wide.region_1.4_spmd.clone.sunk | while | flops 321453056 | bytes 83591480 | solution.py:144
  143.1 1.5 constant_dynamic-slice_fusion.5
  146.9 2.5 fusion.45
  149.4 2.0 copy.118
  152.0 3.0 %fusion.46 = (f32[2,4,64]{2,1,0:T(4,128)S(1)}, f32[2,4,64,1152]{3,2,1,0:T(8,128)S(1)}) fusion(bf16[2,1152,4,128]{3,1,2,0:T(8,128)(2,1)} %bitcast.125, bf16[1,2,64,20,128]{4,2,3,1,0:T(8,128)(2,1)} %get-tuple-element.581, s32[]{:T(128)S(6)} %select_n.105, pred[2,64,1152]{2,1,0:T(8,128)(4,1)S(1)} %copy.119), kind=kOutput, calls=%fused_computation.77.clone.1 | convolution fusion | flops 152763904 | bytes 4999172 | tf_op jit(solution)/shard_map/while/body/eval_jaxpr/tcqhd,tckhd->tchqk/dot_general | solution.py:121
  157.9 1.5 constant_dynamic-slice_fusion.5
  161.6 2.5 fusion.45
  164.2 2.0 copy.118
  166.7 3.0 %fusion.46 = (f32[2,4,64]{2,1,0:T(4,128)S(1)}, f32[2,4,64,1152]{3,2,1,0:T(8,128)S(1)}) fusion(bf16[2,1152,4,128]{3,1,2,0:T(8,128)(2,1)} %bitcast.125, bf16[1,2,64,20,128]{4,2,3,1,0:T(8,128)(2,1)} %get-tuple-element.581, s32[]{:T(128)S(6)} %select_n.105, pred[2,64,1152]{2,1,0:T(8,128)(4,1)S(1)} %copy.119), kind=kOutput, calls=%fused_computation.77.clone.1 | convolution fusion | flops 152763904 | bytes 4999172 | tf_op jit(solution)/shard_map/while/body/eval_jaxpr/tcqhd,tckhd->tchqk/dot_general | solution.py:121
  172.6 1.5 constant_dynamic-slice_fusion.5
  176.4 2.5 fusion.45
  178.9 2.0 copy.118
  181.5 3.0 %fusion.46 = (f32[2,4,64]{2,1,0:T(4,128)S(1)}, f32[2,4,64,1152]{3,2,1,0:T(8,128)S(1)}) fusion(bf16[2,1152,4,128]{3,1,2,0:T(8,128)(2,1)} %bitcast.125, bf16[1,2,64,20,128]{4,2,3,1,0:T(8,128)(2,1)} %get-tuple-element.581, s32[]{:T(128)S(6)} %select_n.105, pred[2,64,1152]{2,1,0:T(8,128)(4,1)S(1)} %copy.119), kind=kOutput, calls=%fused_computation.77.clone.1 | convolution fusion | flops 152763904 | bytes 4999172 | tf_op jit(solution)/shard_map/while/body/eval_jaxpr/tcqhd,tckhd->tchqk/dot_general | solution.py:121
  187.4 1.5 constant_dynamic-slice_fusion.5
  191.2 2.5 fusion.45
  193.7 2.0 copy.118
  196.3 3.0 %fusion.46 = (f32[2,4,64]{2,1,0:T(4,128)S(1)}, f32[2,4,64,1152]{3,2,1,0:T(8,128)S(1)}) fusion(bf16[2,1152,4,128]{3,1,2,0:T(8,128)(2,1)} %bitcast.125, bf16[1,2,64,20,128]{4,2,3,1,0:T(8,128)(2,1)} %get-tuple-element.581, s32[]{:T(128)S(6)} %select_n.105, pred[2,64,1152]{2,1,0:T(8,128)(4,1)S(1)} %copy.119), kind=kOutput, calls=%fused_computation.77.clone.1 | convolution fusion | flops 152763904 | bytes 4999172 | tf_op jit(solution)/shard_map/while/body/eval_jaxpr/tcqhd,tckhd->tchqk/dot_general | solution.py:121
  202.2 1.5 constant_dynamic-slice_fusion.5
  205.9 2.5 fusion.45
  208.5 2.0 copy.118
  211.0 3.0 %fusion.46 = (f32[2,4,64]{2,1,0:T(4,128)S(1)}, f32[2,4,64,1152]{3,2,1,0:T(8,128)S(1)}) fusion(bf16[2,1152,4,128]{3,1,2,0:T(8,128)(2,1)} %bitcast.125, bf16[1,2,64,20,128]{4,2,3,1,0:T(8,128)(2,1)} %get-tuple-element.581, s32[]{:T(128)S(6)} %select_n.105, pred[2,64,1152]{2,1,0:T(8,128)(4,1)S(1)} %copy.119), kind=kOutput, calls=%fused_computation.77.clone.1 | convolution fusion | flops 152763904 | bytes 4999172 | tf_op jit(solution)/shard_map/while/body/eval_jaxpr/tcqhd,tckhd->tchqk/dot_general | solution.py:121
  216.9 37.5 %while.39 = (s32[]{:T(128)}, f32[20,128]{1,0:T(8,128)S(1)}, f32[20,128]{1,0:T(8,128)S(1)}, f32[128,20,128]{0,2,1:T(8,128)}, bf16[2,16,16,2560]{3,2,1,0:T(8,128)(...) while((s32[]{:T(128)}, f32[20,128]{1,0:T(8,128)S(1)}, ...), condition=%wide.region_9.10_spmd.clone, body=%wide.region_6.9_spmd.clone.sunk | while | flops 43929608 | bytes 16578803 | solution.py:177
  217.0 1.2 constant_dynamic-slice_fusion.6
  218.3 1.5 fusion.49
  221.7 1.1 constant_dynamic-slice_fusion.6
  222.9 1.5 fusion.49
  226.4 1.1 constant_dynamic-slice_fusion.6
  227.6 1.5 fusion.49
  231.1 1.1 constant_dynamic-slice_fusion.6
  232.3 1.5 fusion.49
  235.7 1.1 constant_dynamic-slice_fusion.6
  237.0 1.5 fusion.49
  241.6 1.5 fusion.49
  246.3 1.5 fusion.49
  251.0 1.5 fusion.49
  254.5 1.7 divide_convert_fusion
  (245 shorter events, 51.1 us)
Async XLA Ops:
  6.5 62.9 %copy-start = (bf16[4,2,16,2560]{3,2,1,0:T(8,128)(2,1)S(1)}, bf16[4,2,16,2560]{3,2,1,0:T(8,128)(2,1)}, u32[]{:S(2)}) copy-start(bf16[4,2,16,2560]{3,2,1,0:T(8,128)(2,1)} %param.9) | copy-start | bytes 1966084
  6.5 7.4 %copy-start.5 = (bf16[4,2,16,2560]{3,2,1,0:T(8,128)(2,1)S(1)}, bf16[4,2,16,2560]{3,2,1,0:T(8,128)(2,1)}, u32[]{:S(2)}) copy-start(bf16[4,2,16,2560]{3,2,1,0:T(8,128)(2,1)} %param.10) | copy-start | bytes 1966084
  6.5 7.4 %copy-start.6 = (bf16[4,2,16,2560]{3,2,1,0:T(8,128)(2,1)S(1)}, bf16[4,2,16,2560]{3,2,1,0:T(8,128)(2,1)}, u32[]{:S(2)}) copy-start(bf16[4,2,16,2560]{3,2,1,0:T(8,128)(2,1)} %param.11) | copy-start | bytes 1966084
  6.5 64.9 %all-gather.6.cloned.1.call-start = ((), (), s32[]{:S(2)}) async-start(), calls=%async_computation.1 | async-start | bytes 1638400 | tf_op jit(solution)/shard_map/all_gather | solution.py:39
  9.2 48.9 %collective-permute-start = (bf16[2,4,2,16,2560]{4,3,2,1,0:T(8,128)(2,1)}, bf16[2,4,2,16,2560]{4,3,2,1,0:T(8,128)(2,1)S(1)}, u32[]{:S(2)}, u32[]{:S(2)}) collective-permute-start(bf16[2,4,2,16,2560]{4,3,2,1,0:T(8,128)(2,1)} %pad_maximum_fusion.2), channel_id=1, source_target_pairs={{0,8},{8,16},{16,24},{1,9},{9,17},{17,25},{2,10},{10,18},{18,26},{... | collective-permute-start | bytes 3932168 | tf_op jit(solution)/shard_map/ppermute | solution.py:17
  14.8 53.8 %copy-start.8 = (s32[1,1,2,18]{3,2,1,0:T(2,128)S(1)}, s32[1,1,2,18]{3,2,1,0:T(2,128)}, u32[]{:S(2)}) copy-start(s32[1,1,2,18]{3,2,1,0:T(2,128)} %param.12) | copy-start | bytes 436
  14.8 202.2 %all-gather.4.cloned.1.call-start = ((), (), s32[]{:S(2)}) async-start(), calls=%async_computation | async-start | bytes 2949120 | tf_op jit(solution)/shard_map/all_gather | solution.py:154
  59.8 39.0 %collective-permute-start.1 = (bf16[2,8,2,16,2560]{4,3,2,1,0:T(8,128)(2,1)}, bf16[2,8,2,16,2560]{4,3,2,1,0:T(8,128)(2,1)}, u32[]{:S(2)}, u32[]{:S(2)}) collective-permute-start(bf16[2,8,2,16,2560]{4,3,2,1,0:T(8,128)(2,1)} %maximum_maximum_fusion), channel_id=1, source_target_pairs={{0,1},{1,2},{2,3},{3,4},{4,5},{5,6},{6,7},{8,9},{9,10},{10,11},{11... | collective-permute-start | bytes 7864328 | tf_op jit(solution)/shard_map/ppermute | solution.py:28
  66.4 69.2 %collective-permute-start.2 = (bf16[2,8,2,16,2560]{4,3,2,1,0:T(8,128)(2,1)}, bf16[2,8,2,16,2560]{4,3,2,1,0:T(8,128)(2,1)}, u32[]{:S(2)}, u32[]{:S(2)}) collective-permute-start(bf16[2,8,2,16,2560]{4,3,2,1,0:T(8,128)(2,1)} %maximum_maximum_fusion), channel_id=1, source_target_pairs={{1,0},{2,1},{3,2},{4,3},{5,4},{6,5},{7,6},{9,8},{10,9},{11,10},{12... | collective-permute-start | bytes 7864328 | tf_op jit(solution)/shard_map/ppermute | solution.py:30
  152.0 3.0 %copy-start.2 = (bf16[1,1,2,2,4,3,2,3,8,4,128]{10,8,9,2,7,6,5,4,3,1,0:T(8,128)(2,1)S(1)}, bf16[1,1,2,2,4,3,2,3,8,4,128]{10,8,9,2,7,6,5,4,3,1,0:T(8,128)(2,1)}, u32[]{:S(2)}) copy-start(bf16[1,1,2,2,4,3,2,3,8,4,128]{10,8,9,2,7,6,5,4,3,1,0:T(8,128)(2,1)} %get-tuple-element.501) | copy-start | bytes 7077892 | tf_op jit(solution)/shard_map/while
  166.7 3.0 %copy-start.2 = (bf16[1,1,2,2,4,3,2,3,8,4,128]{10,8,9,2,7,6,5,4,3,1,0:T(8,128)(2,1)S(1)}, bf16[1,1,2,2,4,3,2,3,8,4,128]{10,8,9,2,7,6,5,4,3,1,0:T(8,128)(2,1)}, u32[]{:S(2)}) copy-start(bf16[1,1,2,2,4,3,2,3,8,4,128]{10,8,9,2,7,6,5,4,3,1,0:T(8,128)(2,1)} %get-tuple-element.501) | copy-start | bytes 7077892 | tf_op jit(solution)/shard_map/while
  181.5 3.0 %copy-start.2 = (bf16[1,1,2,2,4,3,2,3,8,4,128]{10,8,9,2,7,6,5,4,3,1,0:T(8,128)(2,1)S(1)}, bf16[1,1,2,2,4,3,2,3,8,4,128]{10,8,9,2,7,6,5,4,3,1,0:T(8,128)(2,1)}, u32[]{:S(2)}) copy-start(bf16[1,1,2,2,4,3,2,3,8,4,128]{10,8,9,2,7,6,5,4,3,1,0:T(8,128)(2,1)} %get-tuple-element.501) | copy-start | bytes 7077892 | tf_op jit(solution)/shard_map/while
  196.3 3.0 %copy-start.2 = (bf16[1,1,2,2,4,3,2,3,8,4,128]{10,8,9,2,7,6,5,4,3,1,0:T(8,128)(2,1)S(1)}, bf16[1,1,2,2,4,3,2,3,8,4,128]{10,8,9,2,7,6,5,4,3,1,0:T(8,128)(2,1)}, u32[]{:S(2)}) copy-start(bf16[1,1,2,2,4,3,2,3,8,4,128]{10,8,9,2,7,6,5,4,3,1,0:T(8,128)(2,1)} %get-tuple-element.501) | copy-start | bytes 7077892 | tf_op jit(solution)/shard_map/while
  211.0 3.0 %copy-start.2 = (bf16[1,1,2,2,4,3,2,3,8,4,128]{10,8,9,2,7,6,5,4,3,1,0:T(8,128)(2,1)S(1)}, bf16[1,1,2,2,4,3,2,3,8,4,128]{10,8,9,2,7,6,5,4,3,1,0:T(8,128)(2,1)}, u32[]{:S(2)}) copy-start(bf16[1,1,2,2,4,3,2,3,8,4,128]{10,8,9,2,7,6,5,4,3,1,0:T(8,128)(2,1)} %get-tuple-element.501) | copy-start | bytes 7077892 | tf_op jit(solution)/shard_map/while
  216.9 37.5 %copy-start.7 = (f32[128,20,128]{0,2,1:T(8,128)S(1)}, f32[128,20,128]{0,2,1:T(8,128)}, u32[]{:S(2)}) copy-start(f32[128,20,128]{0,2,1:T(8,128)} %get-tuple-element.295) | copy-start | bytes 3932164
  217.0 3.1 %copy-start.3 = (f32[128,20,128]{0,2,1:T(8,128)S(1)}, f32[128,20,128]{0,2,1:T(8,128)}, u32[]{:S(2)}) copy-start(f32[128,20,128]{0,2,1:T(8,128)} %get-tuple-element.530) | copy-start | bytes 3932164 | tf_op jit(solution)/shard_map/while
  220.6 1.1 copy-start.4
  221.7 3.0 %copy-start.3 = (f32[128,20,128]{0,2,1:T(8,128)S(1)}, f32[128,20,128]{0,2,1:T(8,128)}, u32[]{:S(2)}) copy-start(f32[128,20,128]{0,2,1:T(8,128)} %get-tuple-element.530) | copy-start | bytes 3932164 | tf_op jit(solution)/shard_map/while
  225.3 1.1 copy-start.4
  226.4 3.0 %copy-start.3 = (f32[128,20,128]{0,2,1:T(8,128)S(1)}, f32[128,20,128]{0,2,1:T(8,128)}, u32[]{:S(2)}) copy-start(f32[128,20,128]{0,2,1:T(8,128)} %get-tuple-element.530) | copy-start | bytes 3932164 | tf_op jit(solution)/shard_map/while
  230.0 1.1 copy-start.4
  231.0 3.0 %copy-start.3 = (f32[128,20,128]{0,2,1:T(8,128)S(1)}, f32[128,20,128]{0,2,1:T(8,128)}, u32[]{:S(2)}) copy-start(f32[128,20,128]{0,2,1:T(8,128)} %get-tuple-element.530) | copy-start | bytes 3932164 | tf_op jit(solution)/shard_map/while
  234.6 1.1 copy-start.4
  235.7 3.0 %copy-start.3 = (f32[128,20,128]{0,2,1:T(8,128)S(1)}, f32[128,20,128]{0,2,1:T(8,128)}, u32[]{:S(2)}) copy-start(f32[128,20,128]{0,2,1:T(8,128)} %get-tuple-element.530) | copy-start | bytes 3932164 | tf_op jit(solution)/shard_map/while
  239.3 1.1 copy-start.4
  240.4 3.0 %copy-start.3 = (f32[128,20,128]{0,2,1:T(8,128)S(1)}, f32[128,20,128]{0,2,1:T(8,128)}, u32[]{:S(2)}) copy-start(f32[128,20,128]{0,2,1:T(8,128)} %get-tuple-element.530) | copy-start | bytes 3932164 | tf_op jit(solution)/shard_map/while
  244.0 1.1 copy-start.4
  245.1 3.0 %copy-start.3 = (f32[128,20,128]{0,2,1:T(8,128)S(1)}, f32[128,20,128]{0,2,1:T(8,128)}, u32[]{:S(2)}) copy-start(f32[128,20,128]{0,2,1:T(8,128)} %get-tuple-element.530) | copy-start | bytes 3932164 | tf_op jit(solution)/shard_map/while
  248.7 1.1 copy-start.4
  249.8 3.0 %copy-start.3 = (f32[128,20,128]{0,2,1:T(8,128)S(1)}, f32[128,20,128]{0,2,1:T(8,128)}, u32[]{:S(2)}) copy-start(f32[128,20,128]{0,2,1:T(8,128)} %get-tuple-element.530) | copy-start | bytes 3932164 | tf_op jit(solution)/shard_map/while
  253.4 1.1 copy-start.4
  254.5 3.4 %copy-start.1 = (bf16[4,2,16,2560]{3,2,1,0:T(8,128)(2,1)S(1)}, bf16[4,2,16,2560]{3,2,1,0:T(8,128)(2,1)}, u32[]{:S(2)}) copy-start(bf16[4,2,16,2560]{3,2,1,0:T(8,128)(2,1)} %param.9) | copy-start | bytes 1966084
Sparse Core Ops, SparseCore 0:
  14.9 48.1 all-gather.5
  73.9 44.7 all-gather.3
